TPU v7x, 32 devices: a whole 2x2x4 slice. The times are simulated.
32 devices in a mesh: sub: 4 (over z), wide: 8 (over y, x, core).
Axes of the slice: x: 2, y: 2, z: 4, core: 2. Of those that a mesh axis runs over, the one named last changes fastest.
Arguments:
- load_table: bfloat16 [4, 8, 16, 4, 128], P('sub', 'wide'), may hold values from -6 to 6
- load_column: int32 [64], replicated, may hold values from 0 to 15
- face_order: int32 [4, 8, 4], P('sub', 'wide'), may hold values from 0 to 3, each once within a row
- schur: bfloat16 [4, 8, 512, 512], P('sub', 'wide'), as said below
- neumann: bfloat16 [4, 8, 512, 512], P('sub', 'wide'), as said below
- coarse_basis: bfloat16 [4, 8, 4, 4, 128], P('sub', 'wide'), may hold values from -0.625 to 0.625
- corner_map: int32 [4, 8, 4], P('sub', 'wide'), may hold values from 0 to 47, as said below
- coarse_inverse: float32 [48, 48], P('wide'), as said below
Outputs:
- solution: float32 [4, 8, 4, 64, 128], P('sub', 'wide')
Inputs may be any that keep to these rules, and one draw needn't show every extreme that they name: `corner_map`: each subdomain's 4 entries are distinct; subdomains that meet at a corner of the grid of subdomains give it the same number, and different corners get different numbers, so (5) * (9) of the 48 numbers occur and the others belong to no corner. `coarse_inverse`: Symmetric. `schur`: Symmetric. `neumann`: Symmetric.
All inputs are finite; a program needn't handle non-finite values.
Results may differ from a plain program's by a relative error of at most 0.0014.
Values sent between devices are 32-bit elements; how exact they have to be, the bound alone decides.
A program may use at most 64 MiB of HBM per device.

v0:
```python
import jax
import jax.numpy as jnp
from jax import lax
from jax.sharding import PartitionSpec as P

ITERS = 3
damping = 0.3


def with_halo(cells, sides, width):
    for axis, dim in sides:
        count = lax.axis_size(axis)
        ends = count - 1
        head = lax.slice_in_dim(cells, 0, width, axis=dim)
        tail = lax.slice_in_dim(cells, cells.shape[dim] - width, cells.shape[dim], axis=dim)
        cells = jnp.concatenate(
            [
                lax.ppermute(tail, axis, [(i, (i + 1) % count) for i in range(ends)]),
                cells,
                lax.ppermute(head, axis, [((i + 1) % count, i) for i in range(ends)]),
            ],
            axis=dim,
        )
    return cells


def apply_local(vectors, operators, selector_half, selector_full):
    amount = vectors.shape[0]
    rhs_count = vectors.shape[3]
    face_width = vectors.shape[4]
    rounded = vectors.astype(jnp.bfloat16)
    blocked = jnp.einsum(
        "kcbf,kcfjn->kcjbn", selector_half, rounded, preferred_element_type=jnp.float32
    )
    blocked = blocked.astype(jnp.bfloat16).reshape(amount, 1, rhs_count, 4 * face_width)
    product = jnp.einsum("kcjm,kcmn->kcjn", blocked, operators, preferred_element_type=jnp.float32)
    product = product.reshape(amount, 1, rhs_count, 4, face_width)
    return jnp.einsum("kcbf,kcjbn->kcfjn", selector_full, product, precision=lax.Precision.HIGHEST)


def assemble(copies):
    side_stack = jnp.stack([copies[:, 0, 2], copies[:, 0, 3]], axis=0)
    side_halo = with_halo(side_stack, (("wide", 0),), 1)
    end_stack = jnp.stack([copies[0, 0, 0], copies[-1, 0, 1]], axis=0)
    end_halo = with_halo(end_stack, (("sub", 0),), 1)
    upper_faces = jnp.concatenate([end_halo[0:1], copies[:-1, 0, 1]], axis=0)
    lower_faces = jnp.concatenate([copies[1:, 0, 0], end_halo[3:4]], axis=0)
    north_sum = copies[:, 0, 0] + upper_faces
    south_sum = copies[:, 0, 1] + lower_faces
    west_sum = copies[:, 0, 2] + side_halo[0]
    east_sum = copies[:, 0, 3] + side_halo[3]
    return jnp.stack([north_sum, south_sum, west_sum, east_sum], axis=1)[:, None]


def coarse_solve(partial_value, coarse_inverse):
    assembled = lax.psum(partial_value, ("sub", "wide"))
    owned_rows = jnp.dot(assembled, coarse_inverse.T, precision=lax.Precision.HIGHEST)
    return lax.all_gather(owned_rows, "wide", axis=1, tiled=True)


def body(
    load_table, load_column, face_order, schur, neumann, coarse_basis, corner_map, coarse_inverse
):
    amount = schur.shape[0]
    pattern_count = load_table.shape[2]
    coarse_order = coarse_inverse.shape[1]
    selector_full = (face_order[..., :, None] == jnp.arange(4, dtype=jnp.int32)).astype(jnp.float32)
    selector_half = selector_full.astype(jnp.bfloat16)
    load_select = (load_column[:, None] == jnp.arange(pattern_count, dtype=jnp.int32)).astype(
        jnp.bfloat16
    )
    load_faces = jnp.einsum(
        "jl,kclfn->kcfjn", load_select, load_table, preferred_element_type=jnp.float32
    )
    row_ids = lax.axis_index("sub") * amount + jnp.arange(amount, dtype=jnp.int32)
    rows_total = amount * lax.axis_size("sub")
    column_index = lax.axis_index("wide") * jnp.ones((amount,), jnp.int32)
    cols_total = lax.axis_size("wide")
    half = jnp.float32(0.5)
    whole = jnp.float32(1.0)
    weights = jnp.stack(
        [
            jnp.where(row_ids > 0, half, whole),
            jnp.where(row_ids < rows_total - 1, half, whole),
            jnp.where(column_index > 0, half, whole),
            jnp.where(column_index < cols_total - 1, half, whole),
        ],
        axis=1,
    )[:, None, :, None, None]
    basis = coarse_basis.astype(jnp.float32)
    corner_marks = (corner_map[..., None] == jnp.arange(coarse_order, dtype=jnp.int32)).astype(
        jnp.float32
    )
    solution = jnp.zeros(load_faces.shape, jnp.float32)
    for iteration in range(ITERS):
        if iteration == 0:
            residual = assemble(load_faces)
        else:
            residual = assemble(
                load_faces - apply_local(solution, schur, selector_half, selector_full)
            )
        weighted = weights * residual
        restricted = jnp.einsum(
            "kcpfn,kcfjn->kcpj", basis, weighted, precision=lax.Precision.HIGHEST
        )
        partial_value = jnp.einsum(
            "kcpj,kcpg->jg", restricted, corner_marks, precision=lax.Precision.HIGHEST
        )
        neumann_part = apply_local(weighted, neumann, selector_half, selector_full)
        solved = coarse_solve(partial_value, coarse_inverse)
        picked = jnp.einsum("jg,kcpg->kcpj", solved, corner_marks, precision=lax.Precision.HIGHEST)
        correction = jnp.einsum("kcpj,kcpfn->kcfjn", picked, basis, precision=lax.Precision.HIGHEST)
        update = assemble(weights * (neumann_part + correction))
        solution = solution + damping * update
    return solution


def solution(mesh):
    in_specs = (
        P("sub", "wide", None, None, None),
        P(),
        P("sub", "wide", None),
        P("sub", "wide", None, None),
        P("sub", "wide", None, None),
        P("sub", "wide", None, None, None),
        P("sub", "wide", None),
        P("wide", None),
    )
    out_specs = P("sub", "wide", None, None, None)
    return jax.shard_map(body, mesh=mesh, in_specs=in_specs, out_specs=out_specs, check_vma=False)
```

profile of v0, /device:TPU:4, one launch (start us, length us, event | category | flops | bytes accessed | tf_op | source)
XLA Modules:
  0.0 250.2 jit_solution(4208679977386832550)
XLA Ops:
  0.0 0.7 copy-done
  0.9 3.5 %collective-permute-start = (f32[1,64,128]{2,1,0:T(8,128)S(1)}, f32[1,64,128]{2,1,0:T(8,128)S(1)}, u32[]{:S(2)}, u32[]{:S(2)}) collective-permute-start(f32[1,64,128]{2,1,0:T(8,128)S(1)} %get-tuple-element.47), channel_id=1, source_target_pairs={{0,8},{8,16},{16,24},{1,9},{9,17},{17,25},{2,10},{10,18},{18,26},{... | collective-permute-start | bytes 98312 | tf_op jit(solution)/shard_map/ppermute | solution.py:18
  4.4 1.9 collective-permute-start.2
  6.4 4.5 %collective-permute-start.3 = (f32[1,1,64,128]{3,2,1,0:T(8,128)S(1)}, f32[1,1,64,128]{3,2,1,0:T(8,128)S(1)}, u32[]{:S(2)}, u32[]{:S(2)}) collective-permute-start(f32[1,1,64,128]{3,2,1,0:T(8,128)S(1)} %get-tuple-element.49), channel_id=1, source_target_pairs={{1,0},{2,1},{3,2},{4,3},{5,4},{6,5},{7,6},{9,8},{10,9},{11,10},{12... | collective-permute-start | bytes 98312 | tf_op jit(solution)/shard_map/ppermute | solution.py:20
  10.9 1.3 collective-permute-start.1
  12.3 1.3 copy.133
  13.6 3.1 %collective-permute-done.1 = f32[1,64,128]{2,1,0:T(8,128)S(1)} collective-permute-done((f32[1,64,128]{2,1,0:T(8,128)S(1)}, f32[1,64,128]{2,1,0:T(8,128)S(1)}, u32[]{:S(2)}, u32[]{:S(2)}) %collective-permute-start.1) | collective-permute-done | bytes 32800 | tf_op jit(solution)/shard_map/ppermute | solution.py:20
  16.8 0.6 copy-done.2
  17.6 0.7 copy-done.4
  18.6 0.6 copy-done.6
  19.6 40.5 %psum.21 = f32[64,48]{0,1:T(8,128)S(1)} all-reduce(f32[64,48]{0,1:T(8,128)S(1)} %fusion.44), channel_id=1, replica_groups=mesh['sub'=4,'wide'=8] {'sub','wide'}, use_global_device_ids=true, to_apply=%region_0.1 | all-reduce | flops 3072 | bytes 24576 | tf_op jit(solution)/shard_map/psum | solution.py:56
  60.2 9.0 %all-gather = f32[8,6,64]{2,1,0:T(8,128)S(1)} all-gather(f32[1,6,64]{2,1,0:T(8,128)S(1)} %convolution_bitcast_fusion.6), channel_id=1, replica_groups=mesh['sub'=4,'wide'=8] {'wide'}, dimensions={0}, use_global_device_ids=true | all-gather | bytes 13824 | tf_op jit(solution)/shard_map/all_gather | solution.py:58
  69.4 0.3 fusion.93
  69.7 0.3 fusion.24
  70.4 2.3 collective-permute-start.6
  72.6 4.2 %collective-permute-start.7 = (f32[1,1,64,128]{3,2,1,0:T(8,128)S(1)}, f32[1,1,64,128]{3,2,1,0:T(8,128)S(1)}, u32[]{:S(2)}, u32[]{:S(2)}) collective-permute-start(f32[1,1,64,128]{3,2,1,0:T(8,128)S(1)} %get-tuple-element.41), channel_id=1, source_target_pairs={{1,0},{2,1},{3,2},{4,3},{5,4},{6,5},{7,6},{9,8},{10,9},{11,10},{12... | collective-permute-start | bytes 98312 | tf_op jit(solution)/shard_map/ppermute | solution.py:20
  77.1 2.2 collective-permute-start.4
  79.2 1.3 collective-permute-start.5
  80.8 4.2 %collective-permute-done.5 = f32[1,64,128]{2,1,0:T(8,128)S(1)} collective-permute-done((f32[1,64,128]{2,1,0:T(8,128)S(1)}, f32[1,64,128]{2,1,0:T(8,128)S(1)}, u32[]{:S(2)}, u32[]{:S(2)}) %collective-permute-start.5) | collective-permute-done | bytes 32800 | tf_op jit(solution)/shard_map/ppermute | solution.py:20
  85.6 0.3 fusion.22
  86.0 1.9 collective-permute-start.10
  87.9 4.5 %collective-permute-start.11 = (f32[1,1,64,128]{3,2,1,0:T(8,128)S(1)}, f32[1,1,64,128]{3,2,1,0:T(8,128)S(1)}, u32[]{:S(2)}, u32[]{:S(2)}) collective-permute-start(f32[1,1,64,128]{3,2,1,0:T(8,128)S(1)} %get-tuple-element.33), channel_id=1, source_target_pairs={{1,0},{2,1},{3,2},{4,3},{5,4},{6,5},{7,6},{9,8},{10,9},{11,10},{12... | collective-permute-start | bytes 98312 | tf_op jit(solution)/shard_map/ppermute | solution.py:20
  92.5 3.1 %collective-permute-start.8 = (f32[1,64,128]{2,1,0:T(8,128)S(1)}, f32[1,64,128]{2,1,0:T(8,128)S(1)}, u32[]{:S(2)}, u32[]{:S(2)}) collective-permute-start(f32[1,64,128]{2,1,0:T(8,128)S(1)} %get-tuple-element.31), channel_id=1, source_target_pairs={{0,8},{8,16},{16,24},{1,9},{9,17},{17,25},{2,10},{10,18},{18,26},{... | collective-permute-start | bytes 98312 | tf_op jit(solution)/shard_map/ppermute | solution.py:18
  95.5 1.3 collective-permute-start.9
  97.1 4.2 %collective-permute-done.9 = f32[1,64,128]{2,1,0:T(8,128)S(1)} collective-permute-done((f32[1,64,128]{2,1,0:T(8,128)S(1)}, f32[1,64,128]{2,1,0:T(8,128)S(1)}, u32[]{:S(2)}, u32[]{:S(2)}) %collective-permute-start.9) | collective-permute-done | bytes 32800 | tf_op jit(solution)/shard_map/ppermute | solution.py:20
  102.3 40.3 %psum.22 = f32[64,48]{0,1:T(8,128)S(1)} all-reduce(f32[64,48]{0,1:T(8,128)S(1)} %fusion.43), channel_id=1, replica_groups=mesh['sub'=4,'wide'=8] {'sub','wide'}, use_global_device_ids=true, to_apply=%region_1.2 | all-reduce | flops 3072 | bytes 24576 | tf_op jit(solution)/shard_map/psum | solution.py:56
  142.7 9.5 %all-gather.1 = f32[8,6,64]{2,1,0:T(8,128)S(1)} all-gather(f32[1,6,64]{2,1,0:T(8,128)S(1)} %convolution_bitcast_fusion.5), channel_id=1, replica_groups=mesh['sub'=4,'wide'=8] {'wide'}, dimensions={0}, use_global_device_ids=true | all-gather | bytes 13824 | tf_op jit(solution)/shard_map/all_gather | solution.py:58
  152.7 0.3 fusion.20
  153.3 2.3 collective-permute-start.14
  155.5 4.2 %collective-permute-start.15 = (f32[1,1,64,128]{3,2,1,0:T(8,128)S(1)}, f32[1,1,64,128]{3,2,1,0:T(8,128)S(1)}, u32[]{:S(2)}, u32[]{:S(2)}) collective-permute-start(f32[1,1,64,128]{3,2,1,0:T(8,128)S(1)} %get-tuple-element.25), channel_id=1, source_target_pairs={{1,0},{2,1},{3,2},{4,3},{5,4},{6,5},{7,6},{9,8},{10,9},{11,10},{12... | collective-permute-start | bytes 98312 | tf_op jit(solution)/shard_map/ppermute | solution.py:20
  159.8 1.9 collective-permute-start.12
  161.7 1.3 collective-permute-start.13
  163.3 4.2 %collective-permute-done.13 = f32[1,64,128]{2,1,0:T(8,128)S(1)} collective-permute-done((f32[1,64,128]{2,1,0:T(8,128)S(1)}, f32[1,64,128]{2,1,0:T(8,128)S(1)}, u32[]{:S(2)}, u32[]{:S(2)}) %collective-permute-start.13) | collective-permute-done | bytes 32800 | tf_op jit(solution)/shard_map/ppermute | solution.py:20
  168.1 0.3 fusion.18
  168.5 1.9 collective-permute-start.18
  170.4 4.5 %collective-permute-start.19 = (f32[1,1,64,128]{3,2,1,0:T(8,128)S(1)}, f32[1,1,64,128]{3,2,1,0:T(8,128)S(1)}, u32[]{:S(2)}, u32[]{:S(2)}) collective-permute-start(f32[1,1,64,128]{3,2,1,0:T(8,128)S(1)} %get-tuple-element.17), channel_id=1, source_target_pairs={{1,0},{2,1},{3,2},{4,3},{5,4},{6,5},{7,6},{9,8},{10,9},{11,10},{12... | collective-permute-start | bytes 98312 | tf_op jit(solution)/shard_map/ppermute | solution.py:20
  175.0 2.6 %collective-permute-start.16 = (f32[1,64,128]{2,1,0:T(8,128)S(1)}, f32[1,64,128]{2,1,0:T(8,128)S(1)}, u32[]{:S(2)}, u32[]{:S(2)}) collective-permute-start(f32[1,64,128]{2,1,0:T(8,128)S(1)} %get-tuple-element.15), channel_id=1, source_target_pairs={{0,8},{8,16},{16,24},{1,9},{9,17},{17,25},{2,10},{10,18},{18,26},{... | collective-permute-start | bytes 98312 | tf_op jit(solution)/shard_map/ppermute | solution.py:18
  177.5 1.3 collective-permute-start.17
  179.1 4.2 %collective-permute-done.17 = f32[1,64,128]{2,1,0:T(8,128)S(1)} collective-permute-done((f32[1,64,128]{2,1,0:T(8,128)S(1)}, f32[1,64,128]{2,1,0:T(8,128)S(1)}, u32[]{:S(2)}, u32[]{:S(2)}) %collective-permute-start.17) | collective-permute-done | bytes 32800 | tf_op jit(solution)/shard_map/ppermute | solution.py:20
  184.2 0.3 fusion.16
  184.9 40.3 %psum.23 = f32[64,48]{0,1:T(8,128)S(1)} all-reduce(f32[64,48]{0,1:T(8,128)S(1)} %fusion.42), channel_id=1, replica_groups=mesh['sub'=4,'wide'=8] {'sub','wide'}, use_global_device_ids=true, to_apply=%region_2.3 | all-reduce | flops 3072 | bytes 24576 | tf_op jit(solution)/shard_map/psum | solution.py:56
  225.2 9.5 %all-gather.2 = f32[8,6,64]{2,1,0:T(8,128)S(1)} all-gather(f32[1,6,64]{2,1,0:T(8,128)S(1)} %convolution_bitcast_fusion.4), channel_id=1, replica_groups=mesh['sub'=4,'wide'=8] {'wide'}, dimensions={0}, use_global_device_ids=true | all-gather | bytes 13824 | tf_op jit(solution)/shard_map/all_gather | solution.py:58
  235.3 2.3 collective-permute-start.22
  237.5 4.2 %collective-permute-start.23 = (f32[1,1,64,128]{3,2,1,0:T(8,128)S(1)}, f32[1,1,64,128]{3,2,1,0:T(8,128)S(1)}, u32[]{:S(2)}, u32[]{:S(2)}) collective-permute-start(f32[1,1,64,128]{3,2,1,0:T(8,128)S(1)} %get-tuple-element.9), channel_id=1, source_target_pairs={{1,0},{2,1},{3,2},{4,3},{5,4},{6,5},{7,6},{9,8},{10,9},{11,10},{12... | collective-permute-start | bytes 98312 | tf_op jit(solution)/shard_map/ppermute | solution.py:20
  241.7 1.9 collective-permute-start.20
  243.7 1.3 collective-permute-start.21
  245.2 4.2 %collective-permute-done.21 = f32[1,64,128]{2,1,0:T(8,128)S(1)} collective-permute-done((f32[1,64,128]{2,1,0:T(8,128)S(1)}, f32[1,64,128]{2,1,0:T(8,128)S(1)}, u32[]{:S(2)}, u32[]{:S(2)}) %collective-permute-start.21) | collective-permute-done | bytes 32800 | tf_op jit(solution)/shard_map/ppermute | solution.py:20
  249.5 0.7 fusion.13
  (88 shorter events, 8.0 us)
Async XLA Ops:
  0.0 0.7 copy-start
  0.0 0.7 copy-start.5
  0.9 12.7 %collective-permute-start = (f32[1,64,128]{2,1,0:T(8,128)S(1)}, f32[1,64,128]{2,1,0:T(8,128)S(1)}, u32[]{:S(2)}, u32[]{:S(2)}) collective-permute-start(f32[1,64,128]{2,1,0:T(8,128)S(1)} %get-tuple-element.47), channel_id=1, source_target_pairs={{0,8},{8,16},{16,24},{1,9},{9,17},{17,25},{2,10},{10,18},{18,26},{... | collective-permute-start | bytes 98312 | tf_op jit(solution)/shard_map/ppermute | solution.py:18
  4.4 9.1 %collective-permute-start.2 = (f32[1,1,64,128]{3,2,1,0:T(8,128)S(1)}, f32[1,1,64,128]{3,2,1,0:T(8,128)S(1)}, u32[]{:S(2)}, u32[]{:S(2)}) collective-permute-start(f32[1,1,64,128]{3,2,1,0:T(8,128)S(1)} %get-tuple-element.48), channel_id=1, source_target_pairs={{0,1},{1,2},{2,3},{3,4},{4,5},{5,6},{6,7},{8,9},{9,10},{10,11},{11... | collective-permute-start | bytes 98312 | tf_op jit(solution)/shard_map/ppermute | solution.py:18
  6.4 7.2 %collective-permute-start.3 = (f32[1,1,64,128]{3,2,1,0:T(8,128)S(1)}, f32[1,1,64,128]{3,2,1,0:T(8,128)S(1)}, u32[]{:S(2)}, u32[]{:S(2)}) collective-permute-start(f32[1,1,64,128]{3,2,1,0:T(8,128)S(1)} %get-tuple-element.49), channel_id=1, source_target_pairs={{1,0},{2,1},{3,2},{4,3},{5,4},{6,5},{7,6},{9,8},{10,9},{11,10},{12... | collective-permute-start | bytes 98312 | tf_op jit(solution)/shard_map/ppermute | solution.py:20
  10.9 5.8 %collective-permute-start.1 = (f32[1,64,128]{2,1,0:T(8,128)S(1)}, f32[1,64,128]{2,1,0:T(8,128)S(1)}, u32[]{:S(2)}, u32[]{:S(2)}) collective-permute-start(f32[1,64,128]{2,1,0:T(8,128)S(1)} %get-tuple-element.50), channel_id=1, source_target_pairs={{8,0},{16,8},{24,16},{9,1},{17,9},{25,17},{10,2},{18,10},{26,18},{... | collective-permute-start | bytes 98312 | tf_op jit(solution)/shard_map/ppermute | solution.py:20
  16.7 0.7 copy-start.2
  17.6 0.7 copy-start.4
  18.6 0.7 copy-start.6
  19.5 40.5 %copy-start.3 = (f32[6,48]{1,0:T(8,128)S(1)}, f32[6,48]{1,0:T(8,128)}, u32[]{:S(2)}) copy-start(f32[6,48]{1,0:T(8,128)} %param.15) | copy-start | bytes 3460
  69.7 7.1 %copy-start.1 = (bf16[1,1,512,512]{3,2,1,0:T(8,128)(2,1)S(1)}, bf16[1,1,512,512]{3,2,1,0:T(8,128)(2,1)}, u32[]{:S(2)}) copy-start(bf16[1,1,512,512]{3,2,1,0:T(8,128)(2,1)} %param.11) | copy-start | bytes 1572868
  70.4 10.2 %collective-permute-start.6 = (f32[1,1,64,128]{3,2,1,0:T(8,128)S(1)}, f32[1,1,64,128]{3,2,1,0:T(8,128)S(1)}, u32[]{:S(2)}, u32[]{:S(2)}) collective-permute-start(f32[1,1,64,128]{3,2,1,0:T(8,128)S(1)} %get-tuple-element.40), channel_id=1, source_target_pairs={{0,1},{1,2},{2,3},{3,4},{4,5},{5,6},{6,7},{8,9},{9,10},{10,11},{11... | collective-permute-start | bytes 98312 | tf_op jit(solution)/shard_map/ppermute | solution.py:18
  72.6 7.9 %collective-permute-start.7 = (f32[1,1,64,128]{3,2,1,0:T(8,128)S(1)}, f32[1,1,64,128]{3,2,1,0:T(8,128)S(1)}, u32[]{:S(2)}, u32[]{:S(2)}) collective-permute-start(f32[1,1,64,128]{3,2,1,0:T(8,128)S(1)} %get-tuple-element.41), channel_id=1, source_target_pairs={{1,0},{2,1},{3,2},{4,3},{5,4},{6,5},{7,6},{9,8},{10,9},{11,10},{12... | collective-permute-start | bytes 98312 | tf_op jit(solution)/shard_map/ppermute | solution.py:20
  77.1 3.7 %collective-permute-start.4 = (f32[1,64,128]{2,1,0:T(8,128)S(1)}, f32[1,64,128]{2,1,0:T(8,128)S(1)}, u32[]{:S(2)}, u32[]{:S(2)}) collective-permute-start(f32[1,64,128]{2,1,0:T(8,128)S(1)} %get-tuple-element.39), channel_id=1, source_target_pairs={{0,8},{8,16},{16,24},{1,9},{9,17},{17,25},{2,10},{10,18},{18,26},{... | collective-permute-start | bytes 98312 | tf_op jit(solution)/shard_map/ppermute | solution.py:18
  79.2 5.8 %collective-permute-start.5 = (f32[1,64,128]{2,1,0:T(8,128)S(1)}, f32[1,64,128]{2,1,0:T(8,128)S(1)}, u32[]{:S(2)}, u32[]{:S(2)}) collective-permute-start(f32[1,64,128]{2,1,0:T(8,128)S(1)} %get-tuple-element.42), channel_id=1, source_target_pairs={{8,0},{16,8},{24,16},{9,1},{17,9},{25,17},{10,2},{18,10},{26,18},{... | collective-permute-start | bytes 98312 | tf_op jit(solution)/shard_map/ppermute | solution.py:20
  86.0 10.8 %collective-permute-start.10 = (f32[1,1,64,128]{3,2,1,0:T(8,128)S(1)}, f32[1,1,64,128]{3,2,1,0:T(8,128)S(1)}, u32[]{:S(2)}, u32[]{:S(2)}) collective-permute-start(f32[1,1,64,128]{3,2,1,0:T(8,128)S(1)} %get-tuple-element.32), channel_id=1, source_target_pairs={{0,1},{1,2},{2,3},{3,4},{4,5},{5,6},{6,7},{8,9},{9,10},{10,11},{11... | collective-permute-start | bytes 98312 | tf_op jit(solution)/shard_map/ppermute | solution.py:18
  87.9 8.9 %collective-permute-start.11 = (f32[1,1,64,128]{3,2,1,0:T(8,128)S(1)}, f32[1,1,64,128]{3,2,1,0:T(8,128)S(1)}, u32[]{:S(2)}, u32[]{:S(2)}) collective-permute-start(f32[1,1,64,128]{3,2,1,0:T(8,128)S(1)} %get-tuple-element.33), channel_id=1, source_target_pairs={{1,0},{2,1},{3,2},{4,3},{5,4},{6,5},{7,6},{9,8},{10,9},{11,10},{12... | collective-permute-start | bytes 98312 | tf_op jit(solution)/shard_map/ppermute | solution.py:20
  92.5 4.6 %collective-permute-start.8 = (f32[1,64,128]{2,1,0:T(8,128)S(1)}, f32[1,64,128]{2,1,0:T(8,128)S(1)}, u32[]{:S(2)}, u32[]{:S(2)}) collective-permute-start(f32[1,64,128]{2,1,0:T(8,128)S(1)} %get-tuple-element.31), channel_id=1, source_target_pairs={{0,8},{8,16},{16,24},{1,9},{9,17},{17,25},{2,10},{10,18},{18,26},{... | collective-permute-start | bytes 98312 | tf_op jit(solution)/shard_map/ppermute | solution.py:18
  95.5 5.8 %collective-permute-start.9 = (f32[1,64,128]{2,1,0:T(8,128)S(1)}, f32[1,64,128]{2,1,0:T(8,128)S(1)}, u32[]{:S(2)}, u32[]{:S(2)}) collective-permute-start(f32[1,64,128]{2,1,0:T(8,128)S(1)} %get-tuple-element.34), channel_id=1, source_target_pairs={{8,0},{16,8},{24,16},{9,1},{17,9},{25,17},{10,2},{18,10},{26,18},{... | collective-permute-start | bytes 98312 | tf_op jit(solution)/shard_map/ppermute | solution.py:20
  153.3 9.7 %collective-permute-start.14 = (f32[1,1,64,128]{3,2,1,0:T(8,128)S(1)}, f32[1,1,64,128]{3,2,1,0:T(8,128)S(1)}, u32[]{:S(2)}, u32[]{:S(2)}) collective-permute-start(f32[1,1,64,128]{3,2,1,0:T(8,128)S(1)} %get-tuple-element.24), channel_id=1, source_target_pairs={{0,1},{1,2},{2,3},{3,4},{4,5},{5,6},{6,7},{8,9},{9,10},{10,11},{11... | collective-permute-start | bytes 98312 | tf_op jit(solution)/shard_map/ppermute | solution.py:18
  155.5 7.5 %collective-permute-start.15 = (f32[1,1,64,128]{3,2,1,0:T(8,128)S(1)}, f32[1,1,64,128]{3,2,1,0:T(8,128)S(1)}, u32[]{:S(2)}, u32[]{:S(2)}) collective-permute-start(f32[1,1,64,128]{3,2,1,0:T(8,128)S(1)} %get-tuple-element.25), channel_id=1, source_target_pairs={{1,0},{2,1},{3,2},{4,3},{5,4},{6,5},{7,6},{9,8},{10,9},{11,10},{12... | collective-permute-start | bytes 98312 | tf_op jit(solution)/shard_map/ppermute | solution.py:20
  159.8 3.5 %collective-permute-start.12 = (f32[1,64,128]{2,1,0:T(8,128)S(1)}, f32[1,64,128]{2,1,0:T(8,128)S(1)}, u32[]{:S(2)}, u32[]{:S(2)}) collective-permute-start(f32[1,64,128]{2,1,0:T(8,128)S(1)} %get-tuple-element.23), channel_id=1, source_target_pairs={{0,8},{8,16},{16,24},{1,9},{9,17},{17,25},{2,10},{10,18},{18,26},{... | collective-permute-start | bytes 98312 | tf_op jit(solution)/shard_map/ppermute | solution.py:18
  161.7 5.8 %collective-permute-start.13 = (f32[1,64,128]{2,1,0:T(8,128)S(1)}, f32[1,64,128]{2,1,0:T(8,128)S(1)}, u32[]{:S(2)}, u32[]{:S(2)}) collective-permute-start(f32[1,64,128]{2,1,0:T(8,128)S(1)} %get-tuple-element.26), channel_id=1, source_target_pairs={{8,0},{16,8},{24,16},{9,1},{17,9},{25,17},{10,2},{18,10},{26,18},{... | collective-permute-start | bytes 98312 | tf_op jit(solution)/shard_map/ppermute | solution.py:20
  168.5 10.3 %collective-permute-start.18 = (f32[1,1,64,128]{3,2,1,0:T(8,128)S(1)}, f32[1,1,64,128]{3,2,1,0:T(8,128)S(1)}, u32[]{:S(2)}, u32[]{:S(2)}) collective-permute-start(f32[1,1,64,128]{3,2,1,0:T(8,128)S(1)} %get-tuple-element.16), channel_id=1, source_target_pairs={{0,1},{1,2},{2,3},{3,4},{4,5},{5,6},{6,7},{8,9},{9,10},{10,11},{11... | collective-permute-start | bytes 98312 | tf_op jit(solution)/shard_map/ppermute | solution.py:18
  170.4 8.4 %collective-permute-start.19 = (f32[1,1,64,128]{3,2,1,0:T(8,128)S(1)}, f32[1,1,64,128]{3,2,1,0:T(8,128)S(1)}, u32[]{:S(2)}, u32[]{:S(2)}) collective-permute-start(f32[1,1,64,128]{3,2,1,0:T(8,128)S(1)} %get-tuple-element.17), channel_id=1, source_target_pairs={{1,0},{2,1},{3,2},{4,3},{5,4},{6,5},{7,6},{9,8},{10,9},{11,10},{12... | collective-permute-start | bytes 98312 | tf_op jit(solution)/shard_map/ppermute | solution.py:20
  175.0 4.1 %collective-permute-start.16 = (f32[1,64,128]{2,1,0:T(8,128)S(1)}, f32[1,64,128]{2,1,0:T(8,128)S(1)}, u32[]{:S(2)}, u32[]{:S(2)}) collective-permute-start(f32[1,64,128]{2,1,0:T(8,128)S(1)} %get-tuple-element.15), channel_id=1, source_target_pairs={{0,8},{8,16},{16,24},{1,9},{9,17},{17,25},{2,10},{10,18},{18,26},{... | collective-permute-start | bytes 98312 | tf_op jit(solution)/shard_map/ppermute | solution.py:18
  177.5 5.8 %collective-permute-start.17 = (f32[1,64,128]{2,1,0:T(8,128)S(1)}, f32[1,64,128]{2,1,0:T(8,128)S(1)}, u32[]{:S(2)}, u32[]{:S(2)}) collective-permute-start(f32[1,64,128]{2,1,0:T(8,128)S(1)} %get-tuple-element.18), channel_id=1, source_target_pairs={{8,0},{16,8},{24,16},{9,1},{17,9},{25,17},{10,2},{18,10},{26,18},{... | collective-permute-start | bytes 98312 | tf_op jit(solution)/shard_map/ppermute | solution.py:20
  235.3 9.7 %collective-permute-start.22 = (f32[1,1,64,128]{3,2,1,0:T(8,128)S(1)}, f32[1,1,64,128]{3,2,1,0:T(8,128)S(1)}, u32[]{:S(2)}, u32[]{:S(2)}) collective-permute-start(f32[1,1,64,128]{3,2,1,0:T(8,128)S(1)} %get-tuple-element.8), channel_id=1, source_target_pairs={{0,1},{1,2},{2,3},{3,4},{4,5},{5,6},{6,7},{8,9},{9,10},{10,11},{11... | collective-permute-start | bytes 98312 | tf_op jit(solution)/shard_map/ppermute | solution.py:18
  237.5 7.5 %collective-permute-start.23 = (f32[1,1,64,128]{3,2,1,0:T(8,128)S(1)}, f32[1,1,64,128]{3,2,1,0:T(8,128)S(1)}, u32[]{:S(2)}, u32[]{:S(2)}) collective-permute-start(f32[1,1,64,128]{3,2,1,0:T(8,128)S(1)} %get-tuple-element.9), channel_id=1, source_target_pairs={{1,0},{2,1},{3,2},{4,3},{5,4},{6,5},{7,6},{9,8},{10,9},{11,10},{12... | collective-permute-start | bytes 98312 | tf_op jit(solution)/shard_map/ppermute | solution.py:20
  241.7 3.5 %collective-permute-start.20 = (f32[1,64,128]{2,1,0:T(8,128)S(1)}, f32[1,64,128]{2,1,0:T(8,128)S(1)}, u32[]{:S(2)}, u32[]{:S(2)}) collective-permute-start(f32[1,64,128]{2,1,0:T(8,128)S(1)} %get-tuple-element.7), channel_id=1, source_target_pairs={{0,8},{8,16},{16,24},{1,9},{9,17},{17,25},{2,10},{10,18},{18,26},{... | collective-permute-start | bytes 98312 | tf_op jit(solution)/shard_map/ppermute | solution.py:18
  243.7 5.8 %collective-permute-start.21 = (f32[1,64,128]{2,1,0:T(8,128)S(1)}, f32[1,64,128]{2,1,0:T(8,128)S(1)}, u32[]{:S(2)}, u32[]{:S(2)}) collective-permute-start(f32[1,64,128]{2,1,0:T(8,128)S(1)} %get-tuple-element.10), channel_id=1, source_target_pairs={{8,0},{16,8},{24,16},{9,1},{17,9},{25,17},{10,2},{18,10},{26,18},{... | collective-permute-start | bytes 98312 | tf_op jit(solution)/shard_map/ppermute | solution.py:20
where the time goes:
time: 251 us; the launch traced here: 250 us
  blocking collectives  149 us (59%)
  starting transfers between devices  61.6 us (25%)
  waiting for transfers between devices  25.5 us (10%)
  matrix products  7.57 us (3%)
  local copies, waits for them, and re-layouts  4.4 us (2%)
    psum x3, blocking collectives, coarse_solve(): assembled = lax.psum(partial_value, ('sub', 'wide'))  121 us
    ppermute x12, starting transfers between devices, with_halo(): lax.ppermute(head, axis, [((i + 1) % count, i) for i in range(ends)])  34 us
    all_gather x3, blocking collectives, coarse_solve(): return lax.all_gather(owned_rows, 'wide', axis=1, tiled=True)  28 us
    ppermute x12, starting transfers between devices, with_halo(): lax.ppermute(tail, axis, [(i, (i + 1) % count) for i in range(ends)])  27.6 us
    ppermute x12, waiting for transfers between devices, with_halo(): lax.ppermute(head, axis, [((i + 1) % count, i) for i in range(ends)])  24.3 us
  transfers between devices with their start and end apart: 24, of which 11 were waited for; matrix products, arithmetic and copies ran while one was open for 1% of the time, Pallas kernels for 0%

commit v1 on v0

--- a/solution.py
+++ b/solution.py
@@ -53,7 +53,7 @@
 
 
 def coarse_solve(partial_value, coarse_inverse):
-    assembled = lax.psum(partial_value, ("sub", "wide"))
+    assembled = jnp.sum(lax.all_gather(partial_value, ("sub", "wide")), 0)
     owned_rows = jnp.dot(assembled, coarse_inverse.T, precision=lax.Precision.HIGHEST)
     return lax.all_gather(owned_rows, "wide", axis=1, tiled=True)
 

time: 251 us -> 240 us (0.956)
  blocking collectives: 149 us -> 142 us
  starting transfers between devices: 61.6 us -> 57.1 us
    psum x3 -> x0, blocking collectives: 121 us -> none  [coarse_solve(): assembled = lax.psum(partial_value, ('sub', 'wide'))]
    all_gather x0 -> x3, blocking collectives: none -> 107 us  [coarse_solve(): assembled = jnp.sum(lax.all_gather(partial_value, ('sub', 'wide')), 0)]
    all_gather x3, blocking collectives: 28 us -> 35.4 us  [coarse_solve(): return lax.all_gather(owned_rows, 'wide', axis=1, tiled=True)]
    ppermute x12, starting transfers between devices: 27.6 us -> 23.1 us  [with_halo(): lax.ppermute(tail, axis, [(i, (i + 1) % count) for i in range(ends)])]
where the time goes in v1:
time: 240 us; the launch traced here: 239 us
  blocking collectives  142 us (59%)
  starting transfers between devices  57.1 us (24%)
  waiting for transfers between devices  25.5 us (11%)
  matrix products  7.58 us (3%)
  local copies, waits for them, and re-layouts  5.01 us (2%)
    all_gather x3, blocking collectives, coarse_solve(): assembled = jnp.sum(lax.all_gather(partial_value, ('sub', 'wide')), 0)  107 us
    all_gather x3, blocking collectives, coarse_solve(): return lax.all_gather(owned_rows, 'wide', axis=1, tiled=True)  35.4 us
    ppermute x12, starting transfers between devices, with_halo(): lax.ppermute(head, axis, [((i + 1) % count, i) for i in range(ends)])  34 us
    ppermute x12, waiting for transfers between devices, with_halo(): lax.ppermute(head, axis, [((i + 1) % count, i) for i in range(ends)])  24.3 us
    ppermute x12, starting transfers between devices, with_halo(): lax.ppermute(tail, axis, [(i, (i + 1) % count) for i in range(ends)])  23.1 us
  transfers between devices with their start and end apart: 24, of which 11 were waited for; matrix products, arithmetic and copies ran while one was open for 1% of the time, Pallas kernels for 0%

profile of v1, /device:TPU:4, one launch (start us, length us, event | category | flops | bytes accessed | tf_op | source)
XLA Modules:
  0.0 239.4 jit_solution(16813809174395622771)
XLA Ops:
  0.0 0.7 copy-done
  0.9 3.5 %collective-permute-start = (f32[1,64,128]{2,1,0:T(8,128)S(1)}, f32[1,64,128]{2,1,0:T(8,128)S(1)}, u32[]{:S(2)}, u32[]{:S(2)}) collective-permute-start(f32[1,64,128]{2,1,0:T(8,128)S(1)} %get-tuple-element.47), channel_id=1, source_target_pairs={{0,8},{8,16},{16,24},{1,9},{9,17},{17,25},{2,10},{10,18},{18,26},{... | collective-permute-start | bytes 98312 | tf_op jit(solution)/shard_map/ppermute | solution.py:18
  4.4 1.9 collective-permute-start.2
  6.4 4.5 %collective-permute-start.3 = (f32[1,1,64,128]{3,2,1,0:T(8,128)S(1)}, f32[1,1,64,128]{3,2,1,0:T(8,128)S(1)}, u32[]{:S(2)}, u32[]{:S(2)}) collective-permute-start(f32[1,1,64,128]{3,2,1,0:T(8,128)S(1)} %get-tuple-element.49), channel_id=1, source_target_pairs={{1,0},{2,1},{3,2},{4,3},{5,4},{6,5},{7,6},{9,8},{10,9},{11,10},{12... | collective-permute-start | bytes 98312 | tf_op jit(solution)/shard_map/ppermute | solution.py:20
  10.9 1.3 collective-permute-start.1
  12.3 1.3 copy.133
  13.6 3.1 %collective-permute-done.1 = f32[1,64,128]{2,1,0:T(8,128)S(1)} collective-permute-done((f32[1,64,128]{2,1,0:T(8,128)S(1)}, f32[1,64,128]{2,1,0:T(8,128)S(1)}, u32[]{:S(2)}, u32[]{:S(2)}) %collective-permute-start.1) | collective-permute-done | bytes 32800 | tf_op jit(solution)/shard_map/ppermute | solution.py:20
  16.8 0.6 copy-done.2
  17.6 0.7 copy-done.4
  18.9 0.3 fusion.24
  19.2 0.6 copy-done.6
  20.2 37.6 %all-gather.3 = f32[32,64,48]{1,2,0:T(8,128)S(1)} all-gather(f32[1,64,48]{1,2,0:T(8,128)S(1)} %convolution_bitcast_fusion.6), channel_id=2, replica_groups=mesh['sub'=4,'wide'=8] {'sub','wide'}, dimensions={0}, use_global_device_ids=true | all-gather | bytes 405504 | tf_op jit(solution)/shard_map/all_gather | solution.py:56
  57.8 0.6 copy-done.3
  58.6 11.9 %all-gather.4 = f32[8,6,64]{2,1,0:T(8,128)S(1)} all-gather(f32[1,6,64]{2,1,0:T(8,128)S(1)} %convolution_bitcast_fusion.9), channel_id=1, replica_groups=mesh['sub'=4,'wide'=8] {'wide'}, dimensions={0}, use_global_device_ids=true | all-gather | bytes 13824 | tf_op jit(solution)/shard_map/all_gather | solution.py:58
  71.0 2.3 collective-permute-start.6
  73.2 4.2 %collective-permute-start.7 = (f32[1,1,64,128]{3,2,1,0:T(8,128)S(1)}, f32[1,1,64,128]{3,2,1,0:T(8,128)S(1)}, u32[]{:S(2)}, u32[]{:S(2)}) collective-permute-start(f32[1,1,64,128]{3,2,1,0:T(8,128)S(1)} %get-tuple-element.41), channel_id=1, source_target_pairs={{1,0},{2,1},{3,2},{4,3},{5,4},{6,5},{7,6},{9,8},{10,9},{11,10},{12... | collective-permute-start | bytes 98312 | tf_op jit(solution)/shard_map/ppermute | solution.py:20
  77.7 1.3 collective-permute-start.4
  79.0 1.3 collective-permute-start.5
  80.6 4.2 %collective-permute-done.5 = f32[1,64,128]{2,1,0:T(8,128)S(1)} collective-permute-done((f32[1,64,128]{2,1,0:T(8,128)S(1)}, f32[1,64,128]{2,1,0:T(8,128)S(1)}, u32[]{:S(2)}, u32[]{:S(2)}) %collective-permute-start.5) | collective-permute-done | bytes 32800 | tf_op jit(solution)/shard_map/ppermute | solution.py:20
  85.4 0.3 fusion.22
  85.8 1.9 collective-permute-start.10
  87.7 4.5 %collective-permute-start.11 = (f32[1,1,64,128]{3,2,1,0:T(8,128)S(1)}, f32[1,1,64,128]{3,2,1,0:T(8,128)S(1)}, u32[]{:S(2)}, u32[]{:S(2)}) collective-permute-start(f32[1,1,64,128]{3,2,1,0:T(8,128)S(1)} %get-tuple-element.33), channel_id=1, source_target_pairs={{1,0},{2,1},{3,2},{4,3},{5,4},{6,5},{7,6},{9,8},{10,9},{11,10},{12... | collective-permute-start | bytes 98312 | tf_op jit(solution)/shard_map/ppermute | solution.py:20
  92.2 1.6 collective-permute-start.8
  93.9 1.3 collective-permute-start.9
  95.4 4.2 %collective-permute-done.9 = f32[1,64,128]{2,1,0:T(8,128)S(1)} collective-permute-done((f32[1,64,128]{2,1,0:T(8,128)S(1)}, f32[1,64,128]{2,1,0:T(8,128)S(1)}, u32[]{:S(2)}, u32[]{:S(2)}) %collective-permute-start.9) | collective-permute-done | bytes 32800 | tf_op jit(solution)/shard_map/ppermute | solution.py:20
  100.8 0.3 fusion.20
  101.2 34.5 %all-gather.5 = f32[32,64,48]{1,2,0:T(8,128)S(1)} all-gather(f32[1,64,48]{1,2,0:T(8,128)S(1)} %convolution_bitcast_fusion.5), channel_id=3, replica_groups=mesh['sub'=4,'wide'=8] {'sub','wide'}, dimensions={0}, use_global_device_ids=true | all-gather | bytes 405504 | tf_op jit(solution)/shard_map/all_gather | solution.py:56
  135.9 11.8 %all-gather.6 = f32[8,6,64]{2,1,0:T(8,128)S(1)} all-gather(f32[1,6,64]{2,1,0:T(8,128)S(1)} %convolution_bitcast_fusion.8), channel_id=1, replica_groups=mesh['sub'=4,'wide'=8] {'wide'}, dimensions={0}, use_global_device_ids=true | all-gather | bytes 13824 | tf_op jit(solution)/shard_map/all_gather | solution.py:58
  148.2 2.3 collective-permute-start.14
  150.4 4.2 %collective-permute-start.15 = (f32[1,1,64,128]{3,2,1,0:T(8,128)S(1)}, f32[1,1,64,128]{3,2,1,0:T(8,128)S(1)}, u32[]{:S(2)}, u32[]{:S(2)}) collective-permute-start(f32[1,1,64,128]{3,2,1,0:T(8,128)S(1)} %get-tuple-element.25), channel_id=1, source_target_pairs={{1,0},{2,1},{3,2},{4,3},{5,4},{6,5},{7,6},{9,8},{10,9},{11,10},{12... | collective-permute-start | bytes 98312 | tf_op jit(solution)/shard_map/ppermute | solution.py:20
  154.6 1.3 collective-permute-start.12
  155.9 1.3 collective-permute-start.13
  157.5 4.2 %collective-permute-done.13 = f32[1,64,128]{2,1,0:T(8,128)S(1)} collective-permute-done((f32[1,64,128]{2,1,0:T(8,128)S(1)}, f32[1,64,128]{2,1,0:T(8,128)S(1)}, u32[]{:S(2)}, u32[]{:S(2)}) %collective-permute-start.13) | collective-permute-done | bytes 32800 | tf_op jit(solution)/shard_map/ppermute | solution.py:20
  162.3 0.3 fusion.18
  162.7 1.9 collective-permute-start.18
  164.6 4.5 %collective-permute-start.19 = (f32[1,1,64,128]{3,2,1,0:T(8,128)S(1)}, f32[1,1,64,128]{3,2,1,0:T(8,128)S(1)}, u32[]{:S(2)}, u32[]{:S(2)}) collective-permute-start(f32[1,1,64,128]{3,2,1,0:T(8,128)S(1)} %get-tuple-element.17), channel_id=1, source_target_pairs={{1,0},{2,1},{3,2},{4,3},{5,4},{6,5},{7,6},{9,8},{10,9},{11,10},{12... | collective-permute-start | bytes 98312 | tf_op jit(solution)/shard_map/ppermute | solution.py:20
  169.2 1.6 collective-permute-start.16
  170.8 1.3 collective-permute-start.17
  172.4 4.2 %collective-permute-done.17 = f32[1,64,128]{2,1,0:T(8,128)S(1)} collective-permute-done((f32[1,64,128]{2,1,0:T(8,128)S(1)}, f32[1,64,128]{2,1,0:T(8,128)S(1)}, u32[]{:S(2)}, u32[]{:S(2)}) %collective-permute-start.17) | collective-permute-done | bytes 32800 | tf_op jit(solution)/shard_map/ppermute | solution.py:20
  177.5 0.3 fusion.16
  178.1 34.5 %all-gather.7 = f32[32,64,48]{1,2,0:T(8,128)S(1)} all-gather(f32[1,64,48]{1,2,0:T(8,128)S(1)} %convolution_bitcast_fusion.4), channel_id=4, replica_groups=mesh['sub'=4,'wide'=8] {'sub','wide'}, dimensions={0}, use_global_device_ids=true | all-gather | bytes 405504 | tf_op jit(solution)/shard_map/all_gather | solution.py:56
  212.9 11.8 %all-gather.8 = f32[8,6,64]{2,1,0:T(8,128)S(1)} all-gather(f32[1,6,64]{2,1,0:T(8,128)S(1)} %convolution_bitcast_fusion.7), channel_id=1, replica_groups=mesh['sub'=4,'wide'=8] {'wide'}, dimensions={0}, use_global_device_ids=true | all-gather | bytes 13824 | tf_op jit(solution)/shard_map/all_gather | solution.py:58
  225.1 2.3 collective-permute-start.22
  227.4 4.2 %collective-permute-start.23 = (f32[1,1,64,128]{3,2,1,0:T(8,128)S(1)}, f32[1,1,64,128]{3,2,1,0:T(8,128)S(1)}, u32[]{:S(2)}, u32[]{:S(2)}) collective-permute-start(f32[1,1,64,128]{3,2,1,0:T(8,128)S(1)} %get-tuple-element.9), channel_id=1, source_target_pairs={{1,0},{2,1},{3,2},{4,3},{5,4},{6,5},{7,6},{9,8},{10,9},{11,10},{12... | collective-permute-start | bytes 98312 | tf_op jit(solution)/shard_map/ppermute | solution.py:20
  231.6 1.3 collective-permute-start.20
  232.9 1.3 collective-permute-start.21
  234.5 4.2 %collective-permute-done.21 = f32[1,64,128]{2,1,0:T(8,128)S(1)} collective-permute-done((f32[1,64,128]{2,1,0:T(8,128)S(1)}, f32[1,64,128]{2,1,0:T(8,128)S(1)}, u32[]{:S(2)}, u32[]{:S(2)}) %collective-permute-start.21) | collective-permute-done | bytes 32800 | tf_op jit(solution)/shard_map/ppermute | solution.py:20
  238.7 0.7 fusion.13
  (91 shorter events, 8.5 us)
Async XLA Ops:
  0.0 0.7 copy-start
  0.0 0.7 copy-start.5
  0.9 12.7 %collective-permute-start = (f32[1,64,128]{2,1,0:T(8,128)S(1)}, f32[1,64,128]{2,1,0:T(8,128)S(1)}, u32[]{:S(2)}, u32[]{:S(2)}) collective-permute-start(f32[1,64,128]{2,1,0:T(8,128)S(1)} %get-tuple-element.47), channel_id=1, source_target_pairs={{0,8},{8,16},{16,24},{1,9},{9,17},{17,25},{2,10},{10,18},{18,26},{... | collective-permute-start | bytes 98312 | tf_op jit(solution)/shard_map/ppermute | solution.py:18
  4.4 9.1 %collective-permute-start.2 = (f32[1,1,64,128]{3,2,1,0:T(8,128)S(1)}, f32[1,1,64,128]{3,2,1,0:T(8,128)S(1)}, u32[]{:S(2)}, u32[]{:S(2)}) collective-permute-start(f32[1,1,64,128]{3,2,1,0:T(8,128)S(1)} %get-tuple-element.48), channel_id=1, source_target_pairs={{0,1},{1,2},{2,3},{3,4},{4,5},{5,6},{6,7},{8,9},{9,10},{10,11},{11... | collective-permute-start | bytes 98312 | tf_op jit(solution)/shard_map/ppermute | solution.py:18
  6.4 7.2 %collective-permute-start.3 = (f32[1,1,64,128]{3,2,1,0:T(8,128)S(1)}, f32[1,1,64,128]{3,2,1,0:T(8,128)S(1)}, u32[]{:S(2)}, u32[]{:S(2)}) collective-permute-start(f32[1,1,64,128]{3,2,1,0:T(8,128)S(1)} %get-tuple-element.49), channel_id=1, source_target_pairs={{1,0},{2,1},{3,2},{4,3},{5,4},{6,5},{7,6},{9,8},{10,9},{11,10},{12... | collective-permute-start | bytes 98312 | tf_op jit(solution)/shard_map/ppermute | solution.py:20
  10.9 5.8 %collective-permute-start.1 = (f32[1,64,128]{2,1,0:T(8,128)S(1)}, f32[1,64,128]{2,1,0:T(8,128)S(1)}, u32[]{:S(2)}, u32[]{:S(2)}) collective-permute-start(f32[1,64,128]{2,1,0:T(8,128)S(1)} %get-tuple-element.50), channel_id=1, source_target_pairs={{8,0},{16,8},{24,16},{9,1},{17,9},{25,17},{10,2},{18,10},{26,18},{... | collective-permute-start | bytes 98312 | tf_op jit(solution)/shard_map/ppermute | solution.py:20
  16.7 0.7 copy-start.2
  17.6 0.7 copy-start.4
  19.2 0.7 copy-start.6
  57.8 0.7 copy-start.3
  58.5 19.0 %copy-start.1 = (bf16[1,1,512,512]{3,2,1,0:T(8,128)(2,1)S(1)}, bf16[1,1,512,512]{3,2,1,0:T(8,128)(2,1)}, u32[]{:S(2)}) copy-start(bf16[1,1,512,512]{3,2,1,0:T(8,128)(2,1)} %param.11) | copy-start | bytes 1572868
  71.0 9.3 %collective-permute-start.6 = (f32[1,1,64,128]{3,2,1,0:T(8,128)S(1)}, f32[1,1,64,128]{3,2,1,0:T(8,128)S(1)}, u32[]{:S(2)}, u32[]{:S(2)}) collective-permute-start(f32[1,1,64,128]{3,2,1,0:T(8,128)S(1)} %get-tuple-element.40), channel_id=1, source_target_pairs={{0,1},{1,2},{2,3},{3,4},{4,5},{5,6},{6,7},{8,9},{9,10},{10,11},{11... | collective-permute-start | bytes 98312 | tf_op jit(solution)/shard_map/ppermute | solution.py:18
  73.2 7.1 %collective-permute-start.7 = (f32[1,1,64,128]{3,2,1,0:T(8,128)S(1)}, f32[1,1,64,128]{3,2,1,0:T(8,128)S(1)}, u32[]{:S(2)}, u32[]{:S(2)}) collective-permute-start(f32[1,1,64,128]{3,2,1,0:T(8,128)S(1)} %get-tuple-element.41), channel_id=1, source_target_pairs={{1,0},{2,1},{3,2},{4,3},{5,4},{6,5},{7,6},{9,8},{10,9},{11,10},{12... | collective-permute-start | bytes 98312 | tf_op jit(solution)/shard_map/ppermute | solution.py:20
  77.7 2.9 %collective-permute-start.4 = (f32[1,64,128]{2,1,0:T(8,128)S(1)}, f32[1,64,128]{2,1,0:T(8,128)S(1)}, u32[]{:S(2)}, u32[]{:S(2)}) collective-permute-start(f32[1,64,128]{2,1,0:T(8,128)S(1)} %get-tuple-element.39), channel_id=1, source_target_pairs={{0,8},{8,16},{16,24},{1,9},{9,17},{17,25},{2,10},{10,18},{18,26},{... | collective-permute-start | bytes 98312 | tf_op jit(solution)/shard_map/ppermute | solution.py:18
  79.0 5.8 %collective-permute-start.5 = (f32[1,64,128]{2,1,0:T(8,128)S(1)}, f32[1,64,128]{2,1,0:T(8,128)S(1)}, u32[]{:S(2)}, u32[]{:S(2)}) collective-permute-start(f32[1,64,128]{2,1,0:T(8,128)S(1)} %get-tuple-element.42), channel_id=1, source_target_pairs={{8,0},{16,8},{24,16},{9,1},{17,9},{25,17},{10,2},{18,10},{26,18},{... | collective-permute-start | bytes 98312 | tf_op jit(solution)/shard_map/ppermute | solution.py:20
  85.8 9.4 %collective-permute-start.10 = (f32[1,1,64,128]{3,2,1,0:T(8,128)S(1)}, f32[1,1,64,128]{3,2,1,0:T(8,128)S(1)}, u32[]{:S(2)}, u32[]{:S(2)}) collective-permute-start(f32[1,1,64,128]{3,2,1,0:T(8,128)S(1)} %get-tuple-element.32), channel_id=1, source_target_pairs={{0,1},{1,2},{2,3},{3,4},{4,5},{5,6},{6,7},{8,9},{9,10},{10,11},{11... | collective-permute-start | bytes 98312 | tf_op jit(solution)/shard_map/ppermute | solution.py:18
  87.7 7.5 %collective-permute-start.11 = (f32[1,1,64,128]{3,2,1,0:T(8,128)S(1)}, f32[1,1,64,128]{3,2,1,0:T(8,128)S(1)}, u32[]{:S(2)}, u32[]{:S(2)}) collective-permute-start(f32[1,1,64,128]{3,2,1,0:T(8,128)S(1)} %get-tuple-element.33), channel_id=1, source_target_pairs={{1,0},{2,1},{3,2},{4,3},{5,4},{6,5},{7,6},{9,8},{10,9},{11,10},{12... | collective-permute-start | bytes 98312 | tf_op jit(solution)/shard_map/ppermute | solution.py:20
  92.2 3.2 %collective-permute-start.8 = (f32[1,64,128]{2,1,0:T(8,128)S(1)}, f32[1,64,128]{2,1,0:T(8,128)S(1)}, u32[]{:S(2)}, u32[]{:S(2)}) collective-permute-start(f32[1,64,128]{2,1,0:T(8,128)S(1)} %get-tuple-element.31), channel_id=1, source_target_pairs={{0,8},{8,16},{16,24},{1,9},{9,17},{17,25},{2,10},{10,18},{18,26},{... | collective-permute-start | bytes 98312 | tf_op jit(solution)/shard_map/ppermute | solution.py:18
  93.9 5.8 %collective-permute-start.9 = (f32[1,64,128]{2,1,0:T(8,128)S(1)}, f32[1,64,128]{2,1,0:T(8,128)S(1)}, u32[]{:S(2)}, u32[]{:S(2)}) collective-permute-start(f32[1,64,128]{2,1,0:T(8,128)S(1)} %get-tuple-element.34), channel_id=1, source_target_pairs={{8,0},{16,8},{24,16},{9,1},{17,9},{25,17},{10,2},{18,10},{26,18},{... | collective-permute-start | bytes 98312 | tf_op jit(solution)/shard_map/ppermute | solution.py:20
  148.2 9.1 %collective-permute-start.14 = (f32[1,1,64,128]{3,2,1,0:T(8,128)S(1)}, f32[1,1,64,128]{3,2,1,0:T(8,128)S(1)}, u32[]{:S(2)}, u32[]{:S(2)}) collective-permute-start(f32[1,1,64,128]{3,2,1,0:T(8,128)S(1)} %get-tuple-element.24), channel_id=1, source_target_pairs={{0,1},{1,2},{2,3},{3,4},{4,5},{5,6},{6,7},{8,9},{9,10},{10,11},{11... | collective-permute-start | bytes 98312 | tf_op jit(solution)/shard_map/ppermute | solution.py:18
  150.4 6.8 %collective-permute-start.15 = (f32[1,1,64,128]{3,2,1,0:T(8,128)S(1)}, f32[1,1,64,128]{3,2,1,0:T(8,128)S(1)}, u32[]{:S(2)}, u32[]{:S(2)}) collective-permute-start(f32[1,1,64,128]{3,2,1,0:T(8,128)S(1)} %get-tuple-element.25), channel_id=1, source_target_pairs={{1,0},{2,1},{3,2},{4,3},{5,4},{6,5},{7,6},{9,8},{10,9},{11,10},{12... | collective-permute-start | bytes 98312 | tf_op jit(solution)/shard_map/ppermute | solution.py:20
  154.6 2.9 %collective-permute-start.12 = (f32[1,64,128]{2,1,0:T(8,128)S(1)}, f32[1,64,128]{2,1,0:T(8,128)S(1)}, u32[]{:S(2)}, u32[]{:S(2)}) collective-permute-start(f32[1,64,128]{2,1,0:T(8,128)S(1)} %get-tuple-element.23), channel_id=1, source_target_pairs={{0,8},{8,16},{16,24},{1,9},{9,17},{17,25},{2,10},{10,18},{18,26},{... | collective-permute-start | bytes 98312 | tf_op jit(solution)/shard_map/ppermute | solution.py:18
  155.9 5.8 %collective-permute-start.13 = (f32[1,64,128]{2,1,0:T(8,128)S(1)}, f32[1,64,128]{2,1,0:T(8,128)S(1)}, u32[]{:S(2)}, u32[]{:S(2)}) collective-permute-start(f32[1,64,128]{2,1,0:T(8,128)S(1)} %get-tuple-element.26), channel_id=1, source_target_pairs={{8,0},{16,8},{24,16},{9,1},{17,9},{25,17},{10,2},{18,10},{26,18},{... | collective-permute-start | bytes 98312 | tf_op jit(solution)/shard_map/ppermute | solution.py:20
  162.7 9.4 %collective-permute-start.18 = (f32[1,1,64,128]{3,2,1,0:T(8,128)S(1)}, f32[1,1,64,128]{3,2,1,0:T(8,128)S(1)}, u32[]{:S(2)}, u32[]{:S(2)}) collective-permute-start(f32[1,1,64,128]{3,2,1,0:T(8,128)S(1)} %get-tuple-element.16), channel_id=1, source_target_pairs={{0,1},{1,2},{2,3},{3,4},{4,5},{5,6},{6,7},{8,9},{9,10},{10,11},{11... | collective-permute-start | bytes 98312 | tf_op jit(solution)/shard_map/ppermute | solution.py:18
  164.6 7.5 %collective-permute-start.19 = (f32[1,1,64,128]{3,2,1,0:T(8,128)S(1)}, f32[1,1,64,128]{3,2,1,0:T(8,128)S(1)}, u32[]{:S(2)}, u32[]{:S(2)}) collective-permute-start(f32[1,1,64,128]{3,2,1,0:T(8,128)S(1)} %get-tuple-element.17), channel_id=1, source_target_pairs={{1,0},{2,1},{3,2},{4,3},{5,4},{6,5},{7,6},{9,8},{10,9},{11,10},{12... | collective-permute-start | bytes 98312 | tf_op jit(solution)/shard_map/ppermute | solution.py:20
  169.2 3.2 %collective-permute-start.16 = (f32[1,64,128]{2,1,0:T(8,128)S(1)}, f32[1,64,128]{2,1,0:T(8,128)S(1)}, u32[]{:S(2)}, u32[]{:S(2)}) collective-permute-start(f32[1,64,128]{2,1,0:T(8,128)S(1)} %get-tuple-element.15), channel_id=1, source_target_pairs={{0,8},{8,16},{16,24},{1,9},{9,17},{17,25},{2,10},{10,18},{18,26},{... | collective-permute-start | bytes 98312 | tf_op jit(solution)/shard_map/ppermute | solution.py:18
  170.8 5.8 %collective-permute-start.17 = (f32[1,64,128]{2,1,0:T(8,128)S(1)}, f32[1,64,128]{2,1,0:T(8,128)S(1)}, u32[]{:S(2)}, u32[]{:S(2)}) collective-permute-start(f32[1,64,128]{2,1,0:T(8,128)S(1)} %get-tuple-element.18), channel_id=1, source_target_pairs={{8,0},{16,8},{24,16},{9,1},{17,9},{25,17},{10,2},{18,10},{26,18},{... | collective-permute-start | bytes 98312 | tf_op jit(solution)/shard_map/ppermute | solution.py:20
  225.1 9.1 %collective-permute-start.22 = (f32[1,1,64,128]{3,2,1,0:T(8,128)S(1)}, f32[1,1,64,128]{3,2,1,0:T(8,128)S(1)}, u32[]{:S(2)}, u32[]{:S(2)}) collective-permute-start(f32[1,1,64,128]{3,2,1,0:T(8,128)S(1)} %get-tuple-element.8), channel_id=1, source_target_pairs={{0,1},{1,2},{2,3},{3,4},{4,5},{5,6},{6,7},{8,9},{9,10},{10,11},{11... | collective-permute-start | bytes 98312 | tf_op jit(solution)/shard_map/ppermute | solution.py:18
  227.4 6.8 %collective-permute-start.23 = (f32[1,1,64,128]{3,2,1,0:T(8,128)S(1)}, f32[1,1,64,128]{3,2,1,0:T(8,128)S(1)}, u32[]{:S(2)}, u32[]{:S(2)}) collective-permute-start(f32[1,1,64,128]{3,2,1,0:T(8,128)S(1)} %get-tuple-element.9), channel_id=1, source_target_pairs={{1,0},{2,1},{3,2},{4,3},{5,4},{6,5},{7,6},{9,8},{10,9},{11,10},{12... | collective-permute-start | bytes 98312 | tf_op jit(solution)/shard_map/ppermute | solution.py:20
  231.6 2.9 %collective-permute-start.20 = (f32[1,64,128]{2,1,0:T(8,128)S(1)}, f32[1,64,128]{2,1,0:T(8,128)S(1)}, u32[]{:S(2)}, u32[]{:S(2)}) collective-permute-start(f32[1,64,128]{2,1,0:T(8,128)S(1)} %get-tuple-element.7), channel_id=1, source_target_pairs={{0,8},{8,16},{16,24},{1,9},{9,17},{17,25},{2,10},{10,18},{18,26},{... | collective-permute-start | bytes 98312 | tf_op jit(solution)/shard_map/ppermute | solution.py:18
  232.9 5.8 %collective-permute-start.21 = (f32[1,64,128]{2,1,0:T(8,128)S(1)}, f32[1,64,128]{2,1,0:T(8,128)S(1)}, u32[]{:S(2)}, u32[]{:S(2)}) collective-permute-start(f32[1,64,128]{2,1,0:T(8,128)S(1)} %get-tuple-element.10), channel_id=1, source_target_pairs={{8,0},{16,8},{24,16},{9,1},{17,9},{25,17},{10,2},{18,10},{26,18},{... | collective-permute-start | bytes 98312 | tf_op jit(solution)/shard_map/ppermute | solution.py:20
